TPU v7x, 32 devices: a whole 2x2x4 slice. The times are simulated.
32 devices in a mesh: shots: 2 (over x), slab: 16 (over z, y, core).
Axes of the slice: x: 2, y: 2, z: 4, core: 2. Of those that a mesh axis runs over, the one named last changes fastest.
Arguments:
- fields: float32 [32, 2, 2, 128, 256], P(('shots', 'slab')), parts along dimension 0, may hold values from -6 to 6
- freq_index: int32 [32], P(('shots', 'slab')), parts along dimension 0, may hold values from 0 to 511
- slowness_index: int32 [16, 128, 256], P('slab'), may hold values from 0 to 255
- slowness_table: float32 [256], replicated, may hold values from 1.2 to 2.4
Outputs:
- image: float32 [32, 128, 256], P(('shots', 'slab')), parts along dimension 0
- fields_out: float32 [32, 2, 2, 128, 256], P(('shots', 'slab')), parts along dimension 0
There are 2 independent parts, one for each index of `shots`. A program takes and returns all parts, laid end to end along the dimension named above; an argument that names none is the same for every part. Nothing has to cross between parts.
All inputs are finite; a program needn't handle non-finite values.
Results may differ from a plain program's by a relative error of at most 0.0003.
Values sent between devices are 32-bit elements; how exact they have to be, the bound alone decides.
A program may use at most 64 MiB of HBM per device.

v0:
```python
import functools
import math

import jax
import jax.numpy as jnp
import numpy as np
from jax import lax
from jax.experimental import pallas as pl
from jax.experimental.pallas import tpu as pltpu
from jax.sharding import PartitionSpec as P

TICKS = 3
NFREQ = 512

F32 = jnp.float32
BF16 = jnp.bfloat16
PI_HI = 3.140625
PI_LO = math.pi - 3.140625


def split_np(mat):
    high = mat.astype(BF16)
    low = (mat - high.astype(np.float64)).astype(BF16)
    return high, low


def dft_tables(nx, ny):
    half = ny // 2
    turn = np.outer(np.arange(nx), np.arange(nx)) % nx * (2.0 * np.pi / nx)
    c, s = np.cos(turn), np.sin(turn)
    x_mats = [np.block([[c, s], [-s, c]]), np.block([[c, -s], [s, c]]) / nx]
    y_mats = []
    for odd in (0, 1):
        turn = np.outer(np.arange(half), 2 * np.arange(half) + odd) % ny * (2.0 * np.pi / ny)
        c, s = np.cos(turn), np.sin(turn)
        y_mats.append(np.block([[c, -s], [s, c]]))
        y_mats.append(np.block([[c.T, s.T], [-s.T, c.T]]) / ny)
    xs = np.stack([part for mat in x_mats for part in split_np(mat)])
    ys = np.stack([part for mat in y_mats for part in split_np(mat)])
    return xs, ys


def split(value):
    high = value.astype(BF16)
    low = (value - high.astype(F32)).astype(BF16)
    return high, low


def dot_data_left(data, high, low):
    d_high, d_low = split(data)
    left = jnp.concatenate([d_high, d_low, d_high], axis=1)
    right = jnp.concatenate([high, high, low], axis=0)
    return jnp.dot(left, right, preferred_element_type=F32)


def dot_data_right(high, low, data):
    d_high, d_low = split(data)
    left = jnp.concatenate([high, high, low], axis=1)
    right = jnp.concatenate([d_high, d_low, d_high], axis=0)
    return jnp.dot(left, right, preferred_element_type=F32)


def sincos(x):
    turns = jnp.floor(x * (1.0 / math.pi) + 0.5)
    r = (x - turns * PI_HI) - turns * PI_LO
    sign = 1.0 - 2.0 * (turns - 2.0 * jnp.floor(turns * 0.5))
    r2 = r * r
    sin_p = 1.0 / math.factorial(11) * -1.0
    for k, sg in ((9, 1.0), (7, -1.0), (5, 1.0), (3, -1.0)):
        sin_p = sin_p * r2 + sg / math.factorial(k)
    sin_p = r + r * (r2 * sin_p)
    cos_p = 1.0 / math.factorial(12)
    for k, sg in ((10, -1.0), (8, 1.0), (6, -1.0), (4, 1.0), (2, -1.0), (0, 1.0)):
        cos_p = cos_p * r2 + sg / math.factorial(k)
    return sign * sin_p, sign * cos_p


def kernel(
    count, fields, freq, sidx, table, xs_in, ys_in, image_out, fields_out,
    held, made, plane, index, levels, xs, ys, raw, low, high, omegas,
    in_sems, send_sems, recv_sems, om_send, om_recv, im_send, im_recv,
):
    me = lax.axis_index("slab")
    nx, ny = plane.shape
    half = ny // 2
    has_next = me < count - 1
    has_prev = me > 0
    nxt = jnp.minimum(me + 1, count - 1)
    prv = jnp.maximum(me - 1, 0)

    loads = [
        pltpu.make_async_copy(table, levels, in_sems.at[0]),
        pltpu.make_async_copy(sidx.at[0], index, in_sems.at[1]),
        pltpu.make_async_copy(xs_in, xs, in_sems.at[2]),
        pltpu.make_async_copy(fields.at[0, 0], held.at[0, 0], in_sems.at[3]),
        pltpu.make_async_copy(ys_in, ys, in_sems.at[4]),
        pltpu.make_async_copy(fields.at[0, 1], held.at[0, 1], in_sems.at[5]),
    ]
    for load in loads:
        load.start()

    barrier = pltpu.get_barrier_semaphore()

    @pl.when(has_next)
    def _():
        pl.semaphore_signal(barrier, inc=1, device_id={"slab": nxt})

    @pl.when(has_prev)
    def _():
        pl.semaphore_signal(barrier, inc=1, device_id={"slab": prv})

    def field_copy(tick, f):
        return pltpu.make_async_remote_copy(
            src_ref=made.at[tick, f], dst_ref=held.at[tick + 1, f],
            send_sem=send_sems.at[tick, f], recv_sem=recv_sems.at[tick, f],
            device_id={"slab": nxt},
        )

    def omega_copy(tick):
        return pltpu.make_async_remote_copy(
            src_ref=omegas.at[tick], dst_ref=omegas.at[tick + 1],
            send_sem=om_send.at[tick], recv_sem=om_recv.at[tick],
            device_id={"slab": nxt},
        )

    def image_copy(up):
        return pltpu.make_async_remote_copy(
            src_ref=raw, dst_ref=high if up else low,
            send_sem=im_send.at[up], recv_sem=im_recv.at[up],
            device_id={"slab": prv if up else nxt},
        )

    omegas[0] = jnp.full((8, 128), 1.0 + freq[0].astype(F32) / NFREQ, F32)

    pl.semaphore_wait(barrier, (nxt - me) + (me - prv))

    @pl.when(has_next)
    def _():
        omega_copy(0).start()

    @pl.when(jnp.logical_not(has_prev))
    def _():
        held[1:] = jnp.zeros((TICKS - 1,) + held.shape[1:], F32)
        omegas[1:] = jnp.zeros((TICKS - 1, 8, 128), F32)
        low[...] = jnp.zeros((nx, ny), F32)

    @pl.when(jnp.logical_not(has_next))
    def _():
        high[...] = jnp.zeros((nx, ny), F32)

    loads[0].wait()
    loads[1].wait()
    pieces = [
        jnp.broadcast_to(levels[pl.ds(j * 128, 128)].reshape(1, 128), (nx, 128))
        for j in range(levels.shape[0] // 128)
    ]
    for h in range(ny // 128):
        cols = pl.ds(h * 128, 128)
        idx = index[:, cols]
        inner = idx & 127
        value = jnp.take_along_axis(pieces[0], inner, axis=1, mode="promise_in_bounds")
        for j in range(1, len(pieces)):
            other = jnp.take_along_axis(pieces[j], inner, axis=1, mode="promise_in_bounds")
            value = jnp.where(idx >= j * 128, other, value)
        plane[:, cols] = value
    mean_slow = jnp.sum(plane[...]) * (1.0 / (nx * ny))

    row = lax.broadcasted_iota(jnp.int32, (nx, half), 0)
    wave_x = jnp.where(row < (nx + 1) // 2, row, row - nx).astype(F32) * (2.0 * math.pi / nx)
    lane = lax.broadcasted_iota(jnp.int32, (1, half), 1)

    def phases(omega):
        k_square = (omega * mean_slow) ** 2
        out = []
        for odd in (0, 1):
            k = 2 * lane + odd
            wave_y = jnp.where(k < (ny + 1) // 2, k, k - ny).astype(F32) * (2.0 * math.pi / ny)
            q = k_square - (wave_x * wave_x + wave_y * wave_y)
            root = jnp.sqrt(jnp.abs(q))
            sin_v, cos_v = sincos(root)
            moving = q > 0.0
            out.append((
                jnp.where(moving, cos_v, jnp.exp(-root)),
                jnp.where(moving, sin_v, 0.0),
            ))
        return out

    def step(tick, f, phase, screen):
        re, im = held[tick, f, 0], held[tick, f, 1]
        sg = 1.0 if f == 0 else -1.0
        spec = dot_data_right(xs[0], xs[1], jnp.concatenate([re, im], axis=0))
        left, right = spec[:, :half], spec[:, half:]
        back = []
        for odd, mix in ((0, left + right), (1, left - right)):
            cos_p, sin_p = phase[odd]
            sin_p = sg * sin_p
            fwd = dot_data_left(
                jnp.concatenate([mix[:nx], mix[nx:]], axis=1), ys[4 * odd], ys[4 * odd + 1]
            )
            v_re, v_im = fwd[:, :half], fwd[:, half:]
            moved = jnp.concatenate(
                [v_re * cos_p - v_im * sin_p, v_re * sin_p + v_im * cos_p], axis=1
            )
            back.append(dot_data_left(moved, ys[4 * odd + 2], ys[4 * odd + 3]))
        plus, minus = back[0] + back[1], back[0] - back[1]
        cols = jnp.concatenate([
            jnp.concatenate([plus[:, :half], minus[:, :half]], axis=1),
            jnp.concatenate([plus[:, half:], minus[:, half:]], axis=1),
        ], axis=0)
        field = dot_data_right(xs[2], xs[3], cols)
        b_re, b_im = field[:nx], field[nx:]
        s_sin, s_cos = screen
        s_sin = sg * s_sin
        target = moved_fields(tick)
        target[f, 0] = b_re * s_cos - b_im * s_sin
        target[f, 1] = b_re * s_sin + b_im * s_cos

    def moved_fields(tick):
        return made.at[tick] if tick < TICKS - 1 else fields_out.at[0]

    for tick in range(TICKS):
        if tick > 0:
            @pl.when(has_prev)
            def _():
                omega_copy(tick - 1).wait_recv()

            if tick < TICKS - 1:
                @pl.when(has_next)
                def _():
                    omega_copy(tick).start()
        omega = omegas[tick][:1]
        phase = phases(omega)
        omega_wide = jnp.concatenate([omega] * (ny // 128), axis=1)
        screen = sincos(omega_wide * (plane[...] - mean_slow))
        if tick == 0:
            loads[2].wait()
        for f in (0, 1):
            if tick == 0:
                loads[3 + 2 * f].wait()
                if f == 0:
                    loads[4].wait()
            else:
                @pl.when(has_prev)
                def _():
                    field_copy(tick - 1, f).wait_recv()
            step(tick, f, phase, screen)
            if tick < TICKS - 1:
                @pl.when(has_next)
                def _():
                    field_copy(tick, f).start()
        now = moved_fields(tick)
        added = now[0, 0] * now[1, 0] + now[0, 1] * now[1, 1]
        raw[...] = added if tick == 0 else raw[...] + added

    @pl.when(has_next)
    def _():
        image_copy(0).start()

    @pl.when(has_prev)
    def _():
        image_copy(1).start()

    @pl.when(has_prev)
    def _():
        image_copy(0).wait_recv()

    @pl.when(has_next)
    def _():
        image_copy(1).wait_recv()

    image_out[0] = raw[...] - 0.25 * (low[...] + high[...])

    @pl.when(has_next)
    def _():
        for tick in range(TICKS - 1):
            omega_copy(tick).wait_send()
            for f in (0, 1):
                field_copy(tick, f).wait_send()
        image_copy(0).wait_send()

    @pl.when(has_prev)
    def _():
        image_copy(1).wait_send()


def store(image, fields, image_out, fields_out, sems):
    copies = [
        pltpu.make_async_copy(fields, fields_out, sems.at[0]),
        pltpu.make_async_copy(image, image_out, sems.at[1]),
    ]
    for copy in copies:
        copy.start()
    for copy in copies:
        copy.wait()


def body(fields, freq_index, slowness_index, slowness_table):
    nx, ny = slowness_index.shape[1:]
    assert slowness_index.shape[0] == 1
    xs, ys = dft_tables(nx, ny)
    count = lax.axis_size("slab")
    any_spec = pl.BlockSpec(memory_space=pl.ANY)
    vmem_spec = pl.BlockSpec(memory_space=pltpu.VMEM)
    image, moved = pl.pallas_call(
        functools.partial(kernel, count),
        out_shape=(pltpu.VMEM((1, nx, ny), F32), pltpu.VMEM(fields.shape, F32)),
        in_specs=[
            any_spec, pl.BlockSpec(memory_space=pltpu.SMEM), any_spec, any_spec, any_spec, any_spec,
        ],
        out_specs=(vmem_spec, vmem_spec),
        scratch_shapes=[
            pltpu.VMEM((TICKS, 2, 2, nx, ny), F32),
            pltpu.VMEM((TICKS - 1, 2, 2, nx, ny), F32),
            pltpu.VMEM((nx, ny), F32),
            pltpu.VMEM((nx, ny), jnp.int32),
            pltpu.VMEM(slowness_table.shape, F32),
            pltpu.VMEM(xs.shape, BF16),
            pltpu.VMEM(ys.shape, BF16),
            pltpu.VMEM((nx, ny), F32),
            pltpu.VMEM((nx, ny), F32),
            pltpu.VMEM((nx, ny), F32),
            pltpu.VMEM((TICKS, 8, 128), F32),
            pltpu.SemaphoreType.DMA((6,)),
            pltpu.SemaphoreType.DMA((TICKS - 1, 2)),
            pltpu.SemaphoreType.DMA((TICKS - 1, 2)),
            pltpu.SemaphoreType.DMA((TICKS - 1,)),
            pltpu.SemaphoreType.DMA((TICKS - 1,)),
            pltpu.SemaphoreType.DMA((2,)),
            pltpu.SemaphoreType.DMA((2,)),
        ],
        compiler_params=pltpu.CompilerParams(collective_id=0, has_side_effects=True),
        name="slabs",
    )(fields, freq_index, slowness_index, slowness_table, jnp.asarray(xs), jnp.asarray(ys))
    return pl.pallas_call(
        store,
        out_shape=(
            jax.ShapeDtypeStruct((1, nx, ny), F32),
            jax.ShapeDtypeStruct(fields.shape, F32),
        ),
        in_specs=[vmem_spec, vmem_spec],
        out_specs=(any_spec, any_spec),
        scratch_shapes=[pltpu.SemaphoreType.DMA((2,))],
        name="store",
    )(
        pltpu.with_memory_space_constraint(image, pltpu.VMEM),
        pltpu.with_memory_space_constraint(moved, pltpu.VMEM),
    )


def solution(mesh):
    return jax.shard_map(
        body,
        mesh=mesh,
        in_specs=(
            P(("shots", "slab"), None, None, None, None),
            P(("shots", "slab")),
            P("slab", None, None),
            P(),
        ),
        out_specs=(P(("shots", "slab"), None, None), P(("shots", "slab"), None, None, None, None)),
        check_vma=False,
    )
```

profile of v0, /device:TPU:5, one launch (start us, length us, event | category | flops | bytes accessed | tf_op | source)
XLA Modules:
  0.0 25.1 jit_solution(15156917795986587322)
XLA Ops:
  1.3 23.0 %slabs.1 = (f32[1,128,256]{2,1,0:T(8,128)S(1)}, f32[1,2,2,128,256]{4,3,2,1,0:T(8,128)S(1)}) custom-call(f32[1,2,2,128,256]{4,3,2,1,0:T(8,128)} %fields.1, s32[1]{0:T(128)S(6)} %copy.8.freq, s32[1,128,256]{2,1,0:T(8,128)} %sidx.1, f32[256]{0:T(256)} %table.1, bf16[4,256,256]{2,1,0:T(8,128)(2,1)} %constant.4.clone.xs_in, bf16[8,256,256]{2,1,0:T(8,128)(2,1)} %constant.5.clone.ys_in), custom_call_target="tpu_custom_call" | custom-call | tf_op jit(solution)/shard_map/slabs/pallas_call | solution.py:304
  24.3 0.8 %store.1 = (f32[1,128,256]{2,1,0:T(8,128)}, f32[1,2,2,128,256]{4,3,2,1,0:T(8,128)}) custom-call(f32[1,128,256]{2,1,0:T(8,128)S(1)} %get-tuple-element.4.image, f32[1,2,2,128,256]{4,3,2,1,0:T(8,128)S(1)} %get-tuple-element.5.fields), custom_call_target="tpu_custom_call" | custom-call | tf_op jit(solution)/shard_map/store/pallas_call | solution.py:334
where the time goes:
time: 25.3 us; the launch traced here: 25.1 us
  Pallas kernels  23.8 us (94%)
  between operations  1.28 us (5%)
    pallas_call x1, Pallas kernels, body(): pl.pallas_call(functools.partial(kernel, count), out_shape=(pltpu.VMEM((1...  23 us
    pallas_call x1, Pallas kernels, body(): pl.pallas_call(store, out_shape=(jax.ShapeDtypeStruct((1, nx, ny), F32),...  0.85 us

commit v1 on v0

v1 whole, which is shorter than its diff:
```python
import functools
import math

import jax
import jax.numpy as jnp
import numpy as np
from jax import lax
from jax.experimental import pallas as pl
from jax.experimental.pallas import tpu as pltpu
from jax.sharding import PartitionSpec as P

NFREQ = 512
CHUNKS = 4

F32 = jnp.float32
BF16 = jnp.bfloat16
PI_HI = 3.140625
PI_LO = math.pi - 3.140625


def dft_table(n):
    turn = np.outer(np.arange(n), np.arange(n)) % n * (2.0 * np.pi / n)
    mats = [np.cos(turn), np.sin(turn), -np.sin(turn)]
    high = [mat.astype(BF16) for mat in mats]
    low = [(mat - h.astype(np.float64)).astype(BF16) for mat, h in zip(mats, high)]
    return np.stack(high + low)


def twiddle_table(ny):
    turn = np.arange(ny // 2) * (2.0 * np.pi / ny)
    rows = np.zeros((8, ny // 2), np.float32)
    rows[0], rows[1] = np.cos(turn), np.sin(turn)
    return rows


def split(value):
    high = value.astype(BF16)
    low = (value - high.astype(F32)).astype(BF16)
    return high, low


def cat(values, axis):
    return jnp.concatenate(values, axis=axis)


def block(a, b, c, d):
    return cat([cat([a, b], 1), cat([c, d], 1)], 0)


def dot_data_left(data, high, low):
    d_high, d_low = split(data)
    return jnp.dot(cat([d_high, d_low, d_high], 1), cat([high, high, low], 0), preferred_element_type=F32)


def dot_data_right(high, low, data):
    d_high, d_low = split(data)
    return jnp.dot(cat([high, high, low], 1), cat([d_high, d_low, d_high], 0), preferred_element_type=F32)


def sincos(x):
    turns = jnp.floor(x * (1.0 / math.pi) + 0.5)
    r = (x - turns * PI_HI) - turns * PI_LO
    sign = 1.0 - 2.0 * (turns - 2.0 * jnp.floor(turns * 0.5))
    r2 = r * r
    sin_p = 1.0 / math.factorial(11) * -1.0
    for k, sg in ((9, 1.0), (7, -1.0), (5, 1.0), (3, -1.0)):
        sin_p = sin_p * r2 + sg / math.factorial(k)
    sin_p = r + r * (r2 * sin_p)
    cos_p = 1.0 / math.factorial(12)
    for k, sg in ((10, -1.0), (8, 1.0), (6, -1.0), (4, 1.0), (2, -1.0), (0, 1.0)):
        cos_p = cos_p * r2 + sg / math.factorial(k)
    return sign * sin_p, sign * cos_p


def kernel(
    count, fields, freq, sidx, table, xs_in, ys_in, tw_in, image_out, fields_out,
    own, mid, made, index, planes, levels, xs, ys, tw, wsq, omegas,
    parts_out, parts_in, tail_out, tail_in, sums_out, sums_in,
    in_sems, far_send, far_recv, tile_send, tile_recv, idx_send, idx_recv,
    part_send, part_recv, sum_send, sum_recv,
):
    me = lax.axis_index("slab")
    nx, ny = index.shape[1:]
    half = ny // 2
    rows = nx // CHUNKS
    odd = lax.rem(me, 2) == 1
    even = jnp.logical_not(odd)
    down = me + 2 < count
    up = me >= 2

    def to(offset):
        return {"slab": jnp.clip(me + offset, 0, count - 1)}

    loads = [
        pltpu.make_async_copy(fields.at[0, 0], own.at[0], in_sems.at[0]),
        pltpu.make_async_copy(xs_in, xs, in_sems.at[1]),
        pltpu.make_async_copy(table, levels, in_sems.at[2]),
        pltpu.make_async_copy(sidx.at[0], index.at[0], in_sems.at[3]),
        pltpu.make_async_copy(ys_in, ys, in_sems.at[4]),
        pltpu.make_async_copy(tw_in, tw, in_sems.at[5]),
        pltpu.make_async_copy(fields.at[0, 1], own.at[1], in_sems.at[6]),
    ]
    for load in loads:
        load.start()

    barrier = pltpu.get_barrier_semaphore()

    @pl.when(odd)
    def _():
        pl.semaphore_signal(barrier, inc=1, device_id=to(-1))

        @pl.when(down)
        def _():
            pl.semaphore_signal(barrier, inc=1, device_id=to(1))

    @pl.when(even)
    def _():
        pl.semaphore_signal(barrier, inc=1, device_id=to(1))

        @pl.when(up)
        def _():
            pl.semaphore_signal(barrier, inc=1, device_id=to(-1))

    @pl.when(down)
    def _():
        pl.semaphore_signal(barrier, inc=1, device_id=to(2))

    @pl.when(up)
    def _():
        pl.semaphore_signal(barrier, inc=1, device_id=to(-2))

    row = lax.broadcasted_iota(jnp.int32, (nx, half), 0)
    wave_x = jnp.where(row < (nx + 1) // 2, row, row - nx).astype(F32) * (2.0 * math.pi / nx)
    lane = lax.broadcasted_iota(jnp.int32, (1, half), 1)
    for parity in (0, 1):
        k = 2 * lane + parity
        wave_y = jnp.where(k < (ny + 1) // 2, k, k - ny).astype(F32) * (2.0 * math.pi / ny)
        wsq[pl.ds(parity * nx, nx)] = wave_x * wave_x + wave_y * wave_y

    omegas[0] = jnp.full((8, 128), 1.0 + freq[0].astype(F32) / NFREQ, F32)

    def look_up(slot):
        pieces = [
            jnp.broadcast_to(levels[pl.ds(j * 128, 128)].reshape(1, 128), (nx, 128))
            for j in range(levels.shape[0] // 128)
        ]
        for h in range(ny // 128):
            cols = pl.ds(h * 128, 128)
            idx = index[slot, :, cols]
            inner = idx & 127
            value = jnp.take_along_axis(pieces[0], inner, axis=1, mode="promise_in_bounds")
            for j in range(1, len(pieces)):
                other = jnp.take_along_axis(pieces[j], inner, axis=1, mode="promise_in_bounds")
                value = jnp.where(idx >= j * 128, other, value)
            planes[slot, :, cols] = value
        columns = jnp.sum(planes[slot], axis=0, keepdims=True)
        return jnp.sum(columns, axis=1, keepdims=True) * (1.0 / (nx * ny))

    def factors(omega, slot, mean_slow):
        q = (omega * mean_slow) ** 2 - wsq[...]
        root = jnp.sqrt(jnp.abs(q))
        sin_v, cos_v = sincos(root)
        moving = q > 0.0
        scale = 1.0 / (nx * ny)
        cos_p = jnp.where(moving, cos_v, jnp.exp(-root)) * scale
        sin_p = jnp.where(moving, sin_v, 0.0) * scale
        return (cos_p, sin_p), sincos(omega * (planes[slot] - mean_slow))

    def step(source, target, which, phase, screen):
        x_c, x_s, x_n = ((xs[i], xs[i + 3]) for i in range(3))
        y_c, y_s, y_n = ((ys[i], ys[i + 3]) for i in range(3))
        x_fwd = [block(x_c[i], x_s[i], x_n[i], x_c[i]) for i in (0, 1)]
        x_inv = [block(x_c[i], x_n[i], x_s[i], x_c[i]) for i in (0, 1)]
        y_fwd = [block(y_c[i], y_n[i], y_s[i], y_c[i]) for i in (0, 1)]
        y_inv = [block(y_c[i], y_s[i], y_n[i], y_c[i]) for i in (0, 1)]
        tw_c, tw_s = tw[:1], tw[1:2]
        cos_p, sin_p = phase
        s_sin, s_cos = screen
        mixed = []
        for f in which:
            spec = dot_data_right(*x_fwd, cat([source[f, 0], source[f, 1]], 0))
            left, right = spec[:, :half], spec[:, half:]
            plus, minus = left + right, left - right
            m_re, m_im = minus[:nx], minus[nx:]
            mixed.append(cat([
                cat([plus[:nx], plus[nx:]], 1),
                cat([m_re * tw_c + m_im * tw_s, m_im * tw_c - m_re * tw_s], 1),
            ], 0))
        spectrum = dot_data_left(cat(mixed, 0), *y_fwd)
        shifted = []
        for at, f in enumerate(which):
            v = spectrum[at * 2 * nx:(at + 1) * 2 * nx]
            v_re, v_im = v[:, :half], v[:, half:]
            if f == 0:
                shifted.append(cat([v_re * cos_p - v_im * sin_p, v_re * sin_p + v_im * cos_p], 1))
            else:
                shifted.append(cat([v_re * cos_p + v_im * sin_p, v_im * cos_p - v_re * sin_p], 1))
        back = dot_data_left(cat(shifted, 0), *y_inv)
        for at, f in enumerate(which):
            b = back[at * 2 * nx:(at + 1) * 2 * nx]
            e_re, e_im = b[:nx, :half], b[:nx, half:]
            t_re, t_im = b[nx:, :half], b[nx:, half:]
            o_re, o_im = t_re * tw_c - t_im * tw_s, t_im * tw_c + t_re * tw_s
            moved = dot_data_right(*x_inv, cat([
                cat([e_re + o_re, e_re - o_re], 1), cat([e_im + o_im, e_im - o_im], 1),
            ], 0))
            b_re, b_im = moved[:nx], moved[nx:]
            if f == 0:
                target[f, 0] = b_re * s_cos - b_im * s_sin
                target[f, 1] = b_re * s_sin + b_im * s_cos
            else:
                target[f, 0] = b_re * s_cos + b_im * s_sin
                target[f, 1] = b_im * s_cos - b_re * s_sin

    def product(ref):
        return ref[0, 0] * ref[1, 0] + ref[0, 1] * ref[1, 1]

    def omega_of(slot):
        return omegas[slot, :1, :1]

    def remote(src, dst, send, recv, offset):
        return pltpu.make_async_remote_copy(
            src_ref=src, dst_ref=dst, send_sem=send, recv_sem=recv, device_id=to(offset)
        )

    def field_copy(f):
        return remote(made.at[f], mid.at[f], far_send.at[f], far_recv.at[f], 2)

    def omega_copy():
        return remote(omegas.at[0], omegas.at[1], far_send.at[2], far_recv.at[2], 2)

    def tile_copy(j):
        part = pl.ds(j * rows, rows)
        return remote(
            made.at[:, :, part], fields_out.at[0, :, :, part], tile_send.at[j], tile_recv.at[j], 2
        )

    def index_copy(offset, slot):
        return remote(sidx.at[0], index.at[slot], idx_send.at[slot], idx_recv.at[slot], offset)

    def part_copy(j):
        return remote(parts_out.at[j], parts_in.at[j], part_send.at[j], part_recv.at[j], 1)

    def tail_copy(j):
        part = pl.ds(j * rows, rows)
        return remote(
            tail_out.at[part], tail_in.at[part], part_send.at[3 + j], part_recv.at[3 + j], 1
        )

    def sum_copy(which, slot, offset):
        return remote(sums_out.at[which], sums_in.at[slot], sum_send.at[slot], sum_recv.at[slot], offset)

    @pl.when(odd)
    def _():
        loads[2].wait()
        loads[3].wait()
        mean_own = look_up(0)
        phase, screen = factors(omega_of(0), 0, mean_own)
        for n in (0, 1, 4, 5):
            loads[n].wait()
        step(own, made, (0,), phase, screen)
        pl.semaphore_wait(barrier, 1 + jnp.where(down, 2, 0) + jnp.where(up, 1, 0))

        @pl.when(down)
        def _():
            omega_copy().start()
            field_copy(0).start()

        index_copy(-1, 1).start()
        loads[6].wait()
        step(own, made, (1,), phase, screen)

        @pl.when(down)
        def _():
            field_copy(1).start()

        @pl.when(jnp.logical_not(up))
        def _():
            mid[...] = jnp.zeros(mid.shape, F32)
            omegas[1] = jnp.zeros((8, 128), F32)

        @pl.when(jnp.logical_not(down))
        def _():
            parts_in[2] = jnp.zeros((nx, ny), F32)
            sums_in[2] = jnp.zeros((nx, ny), F32)

        raw = product(made)
        index_copy(1, 1).wait_recv()

        @pl.when(up)
        def _():
            omega_copy().wait_recv()

        mean_low = look_up(1)
        phase_0, screen_0 = factors(omega_of(1), 1, mean_low)
        phase_1, screen_1 = factors(omega_of(1), 0, mean_own)

        @pl.when(up)
        def _():
            field_copy(0).wait_recv()

        step(mid, own, (0,), phase_0, screen_0)
        step(own, fields_out.at[0], (0,), phase_1, screen_1)

        @pl.when(up)
        def _():
            field_copy(1).wait_recv()

        step(mid, own, (1,), phase_0, screen_0)
        part_copy(0).wait_recv()
        sums_out[0] = parts_in[0] + product(own)
        sum_copy(0, 0, -1).start()

        @pl.when(up)
        def _():
            sum_copy(0, 2, -2).start()

        step(own, fields_out.at[0], (1,), phase_1, screen_1)
        part_copy(1).wait_recv()
        sums_out[1] = raw + parts_in[1] + product(fields_out.at[0])
        sum_copy(1, 1, -1).start()

        @pl.when(down)
        def _():
            sum_copy(1, 3, 1).start()
            part_copy(2).wait_recv()
            sum_copy(0, 2, -2).wait_recv()

        image_out[0] = sums_out[1] - 0.25 * (sums_out[0] + parts_in[2] + sums_in[2])

        @pl.when(up)
        def _():
            for j in range(CHUNKS):
                tail_copy(j).wait_recv()
            image_out[0] = image_out[0] - 0.25 * tail_in[...]

        index_copy(-1, 1).wait_send()
        sum_copy(0, 0, -1).wait_send()
        sum_copy(1, 1, -1).wait_send()

        @pl.when(down)
        def _():
            omega_copy().wait_send()
            field_copy(0).wait_send()
            field_copy(1).wait_send()
            sum_copy(1, 3, 1).wait_send()

        @pl.when(up)
        def _():
            sum_copy(0, 2, -2).wait_send()

    @pl.when(even)
    def _():
        pl.semaphore_wait(barrier, 1 + jnp.where(down, 1, 0) + jnp.where(up, 2, 0))

        @pl.when(up)
        def _():
            index_copy(-2, 2).start()

        index_copy(1, 1).start()

        @pl.when(jnp.logical_not(up))
        def _():
            fields_out[0] = jnp.zeros(fields_out.shape[1:], F32)
            sums_in[3] = jnp.zeros((nx, ny), F32)

        loads[2].wait()
        loads[3].wait()
        mean_slow = look_up(0)
        phase, screen = factors(omega_of(0), 0, mean_slow)
        for n in (0, 1, 4, 5, 6):
            loads[n].wait()
        step(own, mid, (0, 1), phase, screen)
        parts_out[0] = product(mid)
        part_copy(0).start()

        index_copy(-1, 1).wait_recv()
        mean_slow = look_up(1)
        phase, screen = factors(omega_of(0), 1, mean_slow)
        step(mid, own, (0, 1), phase, screen)
        parts_out[1] = product(own)
        part_copy(1).start()

        @pl.when(down)
        def _():
            index_copy(-2, 2).wait_recv()
            mean_slow = look_up(2)
            phase, screen = factors(omega_of(0), 2, mean_slow)
            step(own, made, (0, 1), phase, screen)
            for j in range(CHUNKS):
                tile_copy(j).start()
            parts_out[2] = product(made)
            part_copy(2).start()

        sum_copy(0, 0, -1).wait_recv()
        sum_copy(1, 1, -1).wait_recv()
        image_out[0] = sums_in[0] - 0.25 * sums_in[1]

        @pl.when(up)
        def _():
            for j in range(CHUNKS):
                part = pl.ds(j * rows, rows)
                tile_copy(j).wait_recv()
                tail_out[part] = product(fields_out.at[0, :, :, part])
                tail_copy(j).start()
            sum_copy(1, 3, 1).wait_recv()
            image_out[0] = image_out[0] + tail_out[...] - 0.25 * sums_in[3]
            for j in range(CHUNKS):
                tail_copy(j).wait_send()
            index_copy(-2, 2).wait_send()

        index_copy(1, 1).wait_send()
        part_copy(0).wait_send()
        part_copy(1).wait_send()

        @pl.when(down)
        def _():
            for j in range(CHUNKS):
                tile_copy(j).wait_send()
            part_copy(2).wait_send()


def store(image, fields, image_out, fields_out, sems):
    copies = [
        pltpu.make_async_copy(fields, fields_out, sems.at[0]),
        pltpu.make_async_copy(image, image_out, sems.at[1]),
    ]
    for copy in copies:
        copy.start()
    for copy in copies:
        copy.wait()


def body(fields, freq_index, slowness_index, slowness_table):
    nx, ny = slowness_index.shape[1:]
    count = lax.axis_size("slab")
    assert slowness_index.shape[0] == 1 and count % 2 == 0
    half = ny // 2
    xs, ys, tw = dft_table(nx), dft_table(half), twiddle_table(ny)
    any_spec = pl.BlockSpec(memory_space=pl.ANY)
    vmem_spec = pl.BlockSpec(memory_space=pltpu.VMEM)
    plane = (nx, ny)
    dma = pltpu.SemaphoreType.DMA
    image, moved = pl.pallas_call(
        functools.partial(kernel, count),
        out_shape=(pltpu.VMEM((1, nx, ny), F32), pltpu.VMEM(fields.shape, F32)),
        in_specs=[
            any_spec, pl.BlockSpec(memory_space=pltpu.SMEM), any_spec, any_spec,
            any_spec, any_spec, any_spec,
        ],
        out_specs=(vmem_spec, vmem_spec),
        scratch_shapes=[
            pltpu.VMEM((2, 2) + plane, F32),
            pltpu.VMEM((2, 2) + plane, F32),
            pltpu.VMEM((2, 2) + plane, F32),
            pltpu.VMEM((3,) + plane, jnp.int32),
            pltpu.VMEM((3,) + plane, F32),
            pltpu.VMEM(slowness_table.shape, F32),
            pltpu.VMEM(xs.shape, BF16),
            pltpu.VMEM(ys.shape, BF16),
            pltpu.VMEM(tw.shape, F32),
            pltpu.VMEM((2 * nx, half), F32),
            pltpu.VMEM((2, 8, 128), F32),
            pltpu.VMEM((3,) + plane, F32),
            pltpu.VMEM((3,) + plane, F32),
            pltpu.VMEM(plane, F32),
            pltpu.VMEM(plane, F32),
            pltpu.VMEM((2,) + plane, F32),
            pltpu.VMEM((4,) + plane, F32),
            dma((7,)),
            dma((3,)),
            dma((3,)),
            dma((CHUNKS,)),
            dma((CHUNKS,)),
            dma((3,)),
            dma((3,)),
            dma((3 + CHUNKS,)),
            dma((3 + CHUNKS,)),
            dma((4,)),
            dma((4,)),
        ],
        compiler_params=pltpu.CompilerParams(collective_id=0, has_side_effects=True),
        name="slabs",
    )(
        fields, freq_index, slowness_index, slowness_table,
        jnp.asarray(xs), jnp.asarray(ys), jnp.asarray(tw),
    )
    return pl.pallas_call(
        store,
        out_shape=(
            jax.ShapeDtypeStruct((1, nx, ny), F32),
            jax.ShapeDtypeStruct(fields.shape, F32),
        ),
        in_specs=[vmem_spec, vmem_spec],
        out_specs=(any_spec, any_spec),
        scratch_shapes=[dma((2,))],
        name="store",
    )(
        pltpu.with_memory_space_constraint(image, pltpu.VMEM),
        pltpu.with_memory_space_constraint(moved, pltpu.VMEM),
    )


def solution(mesh):
    return jax.shard_map(
        body,
        mesh=mesh,
        in_specs=(
            P(("shots", "slab"), None, None, None, None),
            P(("shots", "slab")),
            P("slab", None, None),
            P(),
        ),
        out_specs=(P(("shots", "slab"), None, None), P(("shots", "slab"), None, None, None, None)),
        check_vma=False,
    )
```

time: 25.3 us -> 33.3 us (1.32)
  the two profiles are of different devices: /device:TPU:5 before, /device:TPU:13 now
where the time goes in v1:
time: 33.3 us; the launch traced here: 33.1 us
  Pallas kernels  31.8 us (95%)
  between operations  1.28 us (4%)
    pallas_call x1, Pallas kernels, body(): pl.pallas_call(functools.partial(kernel, count), out_shape=(pltpu.VMEM((1...  31 us
    pallas_call x1, Pallas kernels, body(): pl.pallas_call(store, out_shape=(jax.ShapeDtypeStruct((1, nx, ny), F32),...  0.85 us

profile of v1, /device:TPU:13, one launch (start us, length us, event | category | flops | bytes accessed | tf_op | source)
XLA Modules:
  0.0 33.1 jit_solution(7648081245211085469)
XLA Ops:
  1.3 31.0 %slabs.1 = (f32[1,128,256]{2,1,0:T(8,128)S(1)}, f32[1,2,2,128,256]{4,3,2,1,0:T(8,128)S(1)}) custom-call(f32[1,2,2,128,256]{4,3,2,1,0:T(8,128)} %fields.1, s32[1]{0:T(128)S(6)} %copy.9.freq, s32[1,128,256]{2,1,0:T(8,128)} %sidx.1, f32[256]{0:T(256)} %table.1, bf16[6,128,128]{2,1,0:T(8,128)(2,1)} %constant.4.clone.xs_in.ys_in, ...), custom_call_target="tpu_custom_call" | custom-call | tf_op jit(solution)/shard_map/slabs/pallas_call | solution.py:444
  32.3 0.8 %store.1 = (f32[1,128,256]{2,1,0:T(8,128)}, f32[1,2,2,128,256]{4,3,2,1,0:T(8,128)}) custom-call(f32[1,128,256]{2,1,0:T(8,128)S(1)} %get-tuple-element.4.image, f32[1,2,2,128,256]{4,3,2,1,0:T(8,128)S(1)} %get-tuple-element.5.fields), custom_call_target="tpu_custom_call" | custom-call | tf_op jit(solution)/shard_map/store/pallas_call | solution.py:488

commit v2 on v1

--- a/solution.py
+++ b/solution.py
@@ -74,10 +74,10 @@
 
 def kernel(
     count, fields, freq, sidx, table, xs_in, ys_in, tw_in, image_out, fields_out,
-    own, mid, made, index, planes, levels, xs, ys, tw, wsq, omegas,
-    parts_out, parts_in, tail_out, tail_in, sums_out, sums_in,
-    in_sems, far_send, far_recv, tile_send, tile_recv, idx_send, idx_recv,
-    part_send, part_recv, sum_send, sum_recv,
+    own, work, made, got, index, planes, levels, xs, ys, tw, wsq, omegas, means, turns,
+    part_out, part_in, raw_out, raw_near, raw_far, first,
+    in_sems, far_send, far_recv, tile_send, tile_recv, pair_send, pair_recv,
+    near_send, near_recv, edge_send, edge_recv,
 ):
     me = lax.axis_index("slab")
     nx, ny = index.shape[1:]
@@ -138,6 +138,15 @@
         wsq[pl.ds(parity * nx, nx)] = wave_x * wave_x + wave_y * wave_y
 
     omegas[0] = jnp.full((8, 128), 1.0 + freq[0].astype(F32) / NFREQ, F32)
+
+    @pl.when(jnp.logical_not(up))
+    def _():
+        got[...] = jnp.zeros(got.shape, F32)
+        omegas[1] = jnp.zeros((8, 128), F32)
+
+    @pl.when(jnp.logical_not(jnp.logical_or(odd & down, even & up)))
+    def _():
+        raw_far[...] = jnp.zeros((nx, ny), F32)
 
     def look_up(slot):
         pieces = [
@@ -156,7 +165,7 @@
         columns = jnp.sum(planes[slot], axis=0, keepdims=True)
         return jnp.sum(columns, axis=1, keepdims=True) * (1.0 / (nx * ny))
 
-    def factors(omega, slot, mean_slow):
+    def phases(omega, mean_slow):
         q = (omega * mean_slow) ** 2 - wsq[...]
         root = jnp.sqrt(jnp.abs(q))
         sin_v, cos_v = sincos(root)
@@ -164,9 +173,12 @@
         scale = 1.0 / (nx * ny)
         cos_p = jnp.where(moving, cos_v, jnp.exp(-root)) * scale
         sin_p = jnp.where(moving, sin_v, 0.0) * scale
-        return (cos_p, sin_p), sincos(omega * (planes[slot] - mean_slow))
-
-    def step(source, target, which, phase, screen):
+        return cos_p, sin_p
+
+    def screens(omega, slot, mean_slow):
+        return sincos(omega * (planes[slot] - mean_slow))
+
+    def spectral(source, which, phase):
         x_c, x_s, x_n = ((xs[i], xs[i + 3]) for i in range(3))
         y_c, y_s, y_n = ((ys[i], ys[i + 3]) for i in range(3))
         x_fwd = [block(x_c[i], x_s[i], x_n[i], x_c[i]) for i in (0, 1)]
@@ -175,7 +187,6 @@
         y_inv = [block(y_c[i], y_s[i], y_n[i], y_c[i]) for i in (0, 1)]
         tw_c, tw_s = tw[:1], tw[1:2]
         cos_p, sin_p = phase
-        s_sin, s_cos = screen
         mixed = []
         for f in which:
             spec = dot_data_right(*x_fwd, cat([source[f, 0], source[f, 1]], 0))
@@ -196,6 +207,7 @@
             else:
                 shifted.append(cat([v_re * cos_p + v_im * sin_p, v_im * cos_p - v_re * sin_p], 1))
         back = dot_data_left(cat(shifted, 0), *y_inv)
+        out = []
         for at, f in enumerate(which):
             b = back[at * 2 * nx:(at + 1) * 2 * nx]
             e_re, e_im = b[:nx, :half], b[:nx, half:]
@@ -204,13 +216,18 @@
             moved = dot_data_right(*x_inv, cat([
                 cat([e_re + o_re, e_re - o_re], 1), cat([e_im + o_im, e_im - o_im], 1),
             ], 0))
-            b_re, b_im = moved[:nx], moved[nx:]
-            if f == 0:
-                target[f, 0] = b_re * s_cos - b_im * s_sin
-                target[f, 1] = b_re * s_sin + b_im * s_cos
-            else:
-                target[f, 0] = b_re * s_cos + b_im * s_sin
-                target[f, 1] = b_im * s_cos - b_re * s_sin
+            out.append((moved[:nx], moved[nx:]))
+        return out
+
+    def turned(f, b_re, b_im, screen):
+        s_sin, s_cos = screen
+        if f == 0:
+            return b_re * s_cos - b_im * s_sin, b_re * s_sin + b_im * s_cos
+        return b_re * s_cos + b_im * s_sin, b_im * s_cos - b_re * s_sin
+
+    def step(source, target, which, phase, screen):
+        for f, (b_re, b_im) in zip(which, spectral(source, which, phase)):
+            target[f, 0], target[f, 1] = turned(f, b_re, b_im, screen)
 
     def product(ref):
         return ref[0, 0] * ref[1, 0] + ref[0, 1] * ref[1, 1]
@@ -224,41 +241,44 @@
         )
 
     def field_copy(f):
-        return remote(made.at[f], mid.at[f], far_send.at[f], far_recv.at[f], 2)
+        return remote(made.at[f], got.at[f], far_send.at[f], far_recv.at[f], 2)
 
     def omega_copy():
         return remote(omegas.at[0], omegas.at[1], far_send.at[2], far_recv.at[2], 2)
+
+    def mean_copy():
+        return remote(means.at[0], means.at[1], far_send.at[3], far_recv.at[3], -2)
 
     def tile_copy(j):
         part = pl.ds(j * rows, rows)
         return remote(
-            made.at[:, :, part], fields_out.at[0, :, :, part], tile_send.at[j], tile_recv.at[j], 2
+            made.at[:, :, part], got.at[:, :, part], tile_send.at[j], tile_recv.at[j], 2
         )
 
-    def index_copy(offset, slot):
-        return remote(sidx.at[0], index.at[slot], idx_send.at[slot], idx_recv.at[slot], offset)
-
-    def part_copy(j):
-        return remote(parts_out.at[j], parts_in.at[j], part_send.at[j], part_recv.at[j], 1)
-
-    def tail_copy(j):
+    def index_copy(offset):
+        return remote(sidx.at[0], index.at[1], pair_send.at[0], pair_recv.at[0], offset)
+
+    def part_copy(offset):
+        return remote(part_out, part_in, pair_send.at[1], pair_recv.at[1], offset)
+
+    def near_copy(j, offset):
         part = pl.ds(j * rows, rows)
-        return remote(
-            tail_out.at[part], tail_in.at[part], part_send.at[3 + j], part_recv.at[3 + j], 1
-        )
-
-    def sum_copy(which, slot, offset):
-        return remote(sums_out.at[which], sums_in.at[slot], sum_send.at[slot], sum_recv.at[slot], offset)
+        return remote(raw_out.at[part], raw_near.at[part], near_send.at[j], near_recv.at[j], offset)
+
+    def edge_copy(j, offset):
+        part = pl.ds(j * rows, rows)
+        return remote(raw_out.at[part], raw_far.at[part], edge_send.at[j], edge_recv.at[j], offset)
+
+    chunks = range(CHUNKS)
 
     @pl.when(odd)
     def _():
-        loads[2].wait()
-        loads[3].wait()
+        for load in loads[:6]:
+            load.wait()
         mean_own = look_up(0)
-        phase, screen = factors(omega_of(0), 0, mean_own)
-        for n in (0, 1, 4, 5):
-            loads[n].wait()
-        step(own, made, (0,), phase, screen)
+        phase = phases(omega_of(0), mean_own)
+        screen_own = screens(omega_of(0), 0, mean_own)
+        step(own, made, (0,), phase, screen_own)
         pl.semaphore_wait(barrier, 1 + jnp.where(down, 2, 0) + jnp.where(up, 1, 0))
 
         @pl.when(down)
@@ -266,158 +286,168 @@
             omega_copy().start()
             field_copy(0).start()
 
-        index_copy(-1, 1).start()
+        index_copy(-1).start()
         loads[6].wait()
-        step(own, made, (1,), phase, screen)
+        step(own, made, (1,), phase, screen_own)
 
         @pl.when(down)
         def _():
             field_copy(1).start()
 
-        @pl.when(jnp.logical_not(up))
-        def _():
-            mid[...] = jnp.zeros(mid.shape, F32)
-            omegas[1] = jnp.zeros((8, 128), F32)
-
-        @pl.when(jnp.logical_not(down))
-        def _():
-            parts_in[2] = jnp.zeros((nx, ny), F32)
-            sums_in[2] = jnp.zeros((nx, ny), F32)
-
-        raw = product(made)
-        index_copy(1, 1).wait_recv()
+        first[...] = product(made)
+        index_copy(1).wait_recv()
 
         @pl.when(up)
         def _():
             omega_copy().wait_recv()
 
         mean_low = look_up(1)
-        phase_0, screen_0 = factors(omega_of(1), 1, mean_low)
-        phase_1, screen_1 = factors(omega_of(1), 0, mean_own)
+        phase_0 = phases(omega_of(1), mean_low)
+        screen_0 = screens(omega_of(1), 1, mean_low)
+        phase_1 = phases(omega_of(1), mean_own)
+        screen_1 = screens(omega_of(1), 0, mean_own)
 
         @pl.when(up)
         def _():
             field_copy(0).wait_recv()
 
-        step(mid, own, (0,), phase_0, screen_0)
-        step(own, fields_out.at[0], (0,), phase_1, screen_1)
+        step(got, work, (0,), phase_0, screen_0)
+        step(work, fields_out.at[0], (0,), phase_1, screen_1)
 
         @pl.when(up)
         def _():
             field_copy(1).wait_recv()
 
-        step(mid, own, (1,), phase_0, screen_0)
-        part_copy(0).wait_recv()
-        sums_out[0] = parts_in[0] + product(own)
-        sum_copy(0, 0, -1).start()
-
-        @pl.when(up)
-        def _():
-            sum_copy(0, 2, -2).start()
-
-        step(own, fields_out.at[0], (1,), phase_1, screen_1)
+        step(got, work, (1,), phase_0, screen_0)
+        part_out[...] = product(work)
+        part_copy(-1).start()
+        step(work, fields_out.at[0], (1,), phase_1, screen_1)
         part_copy(1).wait_recv()
-        sums_out[1] = raw + parts_in[1] + product(fields_out.at[0])
-        sum_copy(1, 1, -1).start()
-
-        @pl.when(down)
-        def _():
-            sum_copy(1, 3, 1).start()
-            part_copy(2).wait_recv()
-            sum_copy(0, 2, -2).wait_recv()
-
-        image_out[0] = sums_out[1] - 0.25 * (sums_out[0] + parts_in[2] + sums_in[2])
-
-        @pl.when(up)
-        def _():
-            for j in range(CHUNKS):
-                tail_copy(j).wait_recv()
-            image_out[0] = image_out[0] - 0.25 * tail_in[...]
-
-        index_copy(-1, 1).wait_send()
-        sum_copy(0, 0, -1).wait_send()
-        sum_copy(1, 1, -1).wait_send()
+        raw_out[...] = first[...] + part_in[...] + product(fields_out.at[0])
+        for j in chunks:
+            near_copy(j, -1).start()
+
+        @pl.when(down)
+        def _():
+            for j in chunks:
+                edge_copy(j, 1).start()
+
+        for j in chunks:
+            part = pl.ds(j * rows, rows)
+            near_copy(j, 1).wait_recv()
+
+            @pl.when(down)
+            def _():
+                edge_copy(j, -1).wait_recv()
+
+            image_out[0, part] = raw_out[part] - 0.25 * (raw_near[part] + raw_far[part])
+
+        index_copy(-1).wait_send()
+        part_copy(-1).wait_send()
+        for j in chunks:
+            near_copy(j, -1).wait_send()
 
         @pl.when(down)
         def _():
             omega_copy().wait_send()
             field_copy(0).wait_send()
             field_copy(1).wait_send()
-            sum_copy(1, 3, 1).wait_send()
-
-        @pl.when(up)
-        def _():
-            sum_copy(0, 2, -2).wait_send()
+            for j in chunks:
+                edge_copy(j, 1).wait_send()
 
     @pl.when(even)
     def _():
+        for load in loads[:6]:
+            load.wait()
+        mean_own = look_up(0)
+        means[0] = jnp.broadcast_to(mean_own, (8, 128))
         pl.semaphore_wait(barrier, 1 + jnp.where(down, 1, 0) + jnp.where(up, 2, 0))
 
         @pl.when(up)
         def _():
-            index_copy(-2, 2).start()
-
-        index_copy(1, 1).start()
-
-        @pl.when(jnp.logical_not(up))
-        def _():
-            fields_out[0] = jnp.zeros(fields_out.shape[1:], F32)
-            sums_in[3] = jnp.zeros((nx, ny), F32)
-
-        loads[2].wait()
-        loads[3].wait()
-        mean_slow = look_up(0)
-        phase, screen = factors(omega_of(0), 0, mean_slow)
-        for n in (0, 1, 4, 5, 6):
-            loads[n].wait()
-        step(own, mid, (0, 1), phase, screen)
-        parts_out[0] = product(mid)
-        part_copy(0).start()
-
-        index_copy(-1, 1).wait_recv()
-        mean_slow = look_up(1)
-        phase, screen = factors(omega_of(0), 1, mean_slow)
-        step(mid, own, (0, 1), phase, screen)
-        parts_out[1] = product(own)
+            mean_copy().start()
+
+        @pl.when(down)
+        def _():
+            omega_copy().start()
+
+        index_copy(1).start()
+        loads[6].wait()
+        phase = phases(omega_of(0), mean_own)
+        screen = screens(omega_of(0), 0, mean_own)
+        step(own, work, (0, 1), phase, screen)
+        first[...] = product(work)
+
+        index_copy(-1).wait_recv()
+        mean_next = look_up(1)
+        phase = phases(omega_of(0), mean_next)
+        screen = screens(omega_of(0), 1, mean_next)
+        step(work, own, (0, 1), phase, screen)
+        part_out[...] = product(own)
         part_copy(1).start()
 
         @pl.when(down)
         def _():
-            index_copy(-2, 2).wait_recv()
-            mean_slow = look_up(2)
-            phase, screen = factors(omega_of(0), 2, mean_slow)
-            step(own, made, (0, 1), phase, screen)
-            for j in range(CHUNKS):
+            mean_copy().wait_recv()
+            phase = phases(omega_of(0), means[1, :1, :1])
+            for f, (b_re, b_im) in zip((0, 1), spectral(own, (0, 1), phase)):
+                made[f, 0], made[f, 1] = b_re, b_im
+            for j in chunks:
                 tile_copy(j).start()
-            parts_out[2] = product(made)
-            part_copy(2).start()
-
-        sum_copy(0, 0, -1).wait_recv()
-        sum_copy(1, 1, -1).wait_recv()
-        image_out[0] = sums_in[0] - 0.25 * sums_in[1]
-
-        @pl.when(up)
-        def _():
-            for j in range(CHUNKS):
-                part = pl.ds(j * rows, rows)
+
+        @pl.when(up)
+        def _():
+            omega_copy().wait_recv()
+
+        turns[0], turns[1] = screens(omega_of(1), 0, means[0, :1, :1])
+        part_copy(-1).wait_recv()
+        first[...] = first[...] + part_in[...]
+
+        for j in chunks:
+            part = pl.ds(j * rows, rows)
+
+            @pl.when(up)
+            def _():
                 tile_copy(j).wait_recv()
-                tail_out[part] = product(fields_out.at[0, :, :, part])
-                tail_copy(j).start()
-            sum_copy(1, 3, 1).wait_recv()
-            image_out[0] = image_out[0] + tail_out[...] - 0.25 * sums_in[3]
-            for j in range(CHUNKS):
-                tail_copy(j).wait_send()
-            index_copy(-2, 2).wait_send()
-
-        index_copy(1, 1).wait_send()
-        part_copy(0).wait_send()
+
+            screen = turns[0, part], turns[1, part]
+            s_re, s_im = turned(0, got[0, 0, part], got[0, 1, part], screen)
+            r_re, r_im = turned(1, got[1, 0, part], got[1, 1, part], screen)
+            raw_out[part] = first[part] + s_re * r_re + s_im * r_im
+            fields_out[0, 0, 0, part], fields_out[0, 0, 1, part] = s_re, s_im
+            fields_out[0, 1, 0, part], fields_out[0, 1, 1, part] = r_re, r_im
+            near_copy(j, 1).start()
+
+            @pl.when(up)
+            def _():
+                edge_copy(j, -1).start()
+
+        for j in chunks:
+            part = pl.ds(j * rows, rows)
+            near_copy(j, -1).wait_recv()
+
+            @pl.when(up)
+            def _():
+                edge_copy(j, 1).wait_recv()
+
+            image_out[0, part] = raw_out[part] - 0.25 * (raw_near[part] + raw_far[part])
+
+        index_copy(1).wait_send()
         part_copy(1).wait_send()
-
-        @pl.when(down)
-        def _():
-            for j in range(CHUNKS):
+        for j in chunks:
+            near_copy(j, 1).wait_send()
+
+        @pl.when(down)
+        def _():
+            omega_copy().wait_send()
+            for j in chunks:
                 tile_copy(j).wait_send()
-            part_copy(2).wait_send()
+
+        @pl.when(up)
+        def _():
+            mean_copy().wait_send()
+            for j in chunks:
+                edge_copy(j, -1).wait_send()
 
 
 def store(image, fields, image_out, fields_out, sems):
@@ -453,31 +483,34 @@
             pltpu.VMEM((2, 2) + plane, F32),
             pltpu.VMEM((2, 2) + plane, F32),
             pltpu.VMEM((2, 2) + plane, F32),
-            pltpu.VMEM((3,) + plane, jnp.int32),
-            pltpu.VMEM((3,) + plane, F32),
+            pltpu.VMEM((2, 2) + plane, F32),
+            pltpu.VMEM((2,) + plane, jnp.int32),
+            pltpu.VMEM((2,) + plane, F32),
             pltpu.VMEM(slowness_table.shape, F32),
             pltpu.VMEM(xs.shape, BF16),
             pltpu.VMEM(ys.shape, BF16),
             pltpu.VMEM(tw.shape, F32),
             pltpu.VMEM((2 * nx, half), F32),
             pltpu.VMEM((2, 8, 128), F32),
-            pltpu.VMEM((3,) + plane, F32),
-            pltpu.VMEM((3,) + plane, F32),
+            pltpu.VMEM((2, 8, 128), F32),
+            pltpu.VMEM((2,) + plane, F32),
             pltpu.VMEM(plane, F32),
             pltpu.VMEM(plane, F32),
-            pltpu.VMEM((2,) + plane, F32),
-            pltpu.VMEM((4,) + plane, F32),
+            pltpu.VMEM(plane, F32),
+            pltpu.VMEM(plane, F32),
+            pltpu.VMEM(plane, F32),
+            pltpu.VMEM(plane, F32),
             dma((7,)),
-            dma((3,)),
-            dma((3,)),
+            dma((4,)),
+            dma((4,)),
             dma((CHUNKS,)),
             dma((CHUNKS,)),
-            dma((3,)),
-            dma((3,)),
-            dma((3 + CHUNKS,)),
-            dma((3 + CHUNKS,)),
-            dma((4,)),
-            dma((4,)),
+            dma((2,)),
+            dma((2,)),
+            dma((CHUNKS,)),
+            dma((CHUNKS,)),
+            dma((CHUNKS,)),
+            dma((CHUNKS,)),
         ],
         compiler_params=pltpu.CompilerParams(collective_id=0, has_side_effects=True),
         name="slabs",

time: 33.3 us -> 23.7 us (0.71)
  the two profiles are of different devices: /device:TPU:13 before, /device:TPU:5 now
where the time goes in v2:
time: 23.7 us; the launch traced here: 23.4 us
  Pallas kernels  22.1 us (93%)
  between operations  1.28 us (5%)
    pallas_call x1, Pallas kernels, body(): pl.pallas_call(functools.partial(kernel, count), out_shape=(pltpu.VMEM((1...  21.2 us
    pallas_call x1, Pallas kernels, body(): pl.pallas_call(store, out_shape=(jax.ShapeDtypeStruct((1, nx, ny), F32),...  0.85 us

profile of v2, /device:TPU:5, one launch (start us, length us, event | category | flops | bytes accessed | tf_op | source)
XLA Modules:
  0.0 23.4 jit_solution(5115809640612279874)
XLA Ops:
  1.3 21.2 %slabs.1 = (f32[1,128,256]{2,1,0:T(8,128)S(1)}, f32[1,2,2,128,256]{4,3,2,1,0:T(8,128)S(1)}) custom-call(f32[1,2,2,128,256]{4,3,2,1,0:T(8,128)} %fields.1, s32[1]{0:T(128)S(6)} %copy.9.freq, s32[1,128,256]{2,1,0:T(8,128)} %sidx.1, f32[256]{0:T(256)} %table.1, bf16[6,128,128]{2,1,0:T(8,128)(2,1)} %constant.4.clone.xs_in.ys_in, ...), custom_call_target="tpu_custom_call" | custom-call | tf_op jit(solution)/shard_map/slabs/pallas_call | solution.py:474
  22.5 0.8 %store.1 = (f32[1,128,256]{2,1,0:T(8,128)}, f32[1,2,2,128,256]{4,3,2,1,0:T(8,128)}) custom-call(f32[1,128,256]{2,1,0:T(8,128)S(1)} %get-tuple-element.4.image, f32[1,2,2,128,256]{4,3,2,1,0:T(8,128)S(1)} %get-tuple-element.5.fields), custom_call_target="tpu_custom_call" | custom-call | tf_op jit(solution)/shard_map/store/pallas_call | solution.py:521

commit v3 on v2

--- a/solution.py
+++ b/solution.py
@@ -10,7 +10,8 @@
 from jax.sharding import PartitionSpec as P
 
 NFREQ = 512
-CHUNKS = 4
+SHARES = (3, 2, 2, 1)
+CHUNKS = len(SHARES)
 
 F32 = jnp.float32
 BF16 = jnp.bfloat16
@@ -82,7 +83,12 @@
     me = lax.axis_index("slab")
     nx, ny = index.shape[1:]
     half = ny // 2
-    rows = nx // CHUNKS
+    unit = nx // sum(SHARES)
+    starts = [unit * sum(SHARES[:j]) for j in range(CHUNKS)]
+
+    def part_of(j):
+        return pl.ds(starts[j], unit * SHARES[j])
+
     odd = lax.rem(me, 2) == 1
     even = jnp.logical_not(odd)
     down = me + 2 < count
@@ -250,9 +256,9 @@
         return remote(means.at[0], means.at[1], far_send.at[3], far_recv.at[3], -2)
 
     def tile_copy(j):
-        part = pl.ds(j * rows, rows)
+        part = part_of(j)
         return remote(
-            made.at[:, :, part], got.at[:, :, part], tile_send.at[j], tile_recv.at[j], 2
+            made.at[1, :, part], got.at[1, :, part], tile_send.at[j], tile_recv.at[j], 2
         )
 
     def index_copy(offset):
@@ -262,12 +268,15 @@
         return remote(part_out, part_in, pair_send.at[1], pair_recv.at[1], offset)
 
     def near_copy(j, offset):
-        part = pl.ds(j * rows, rows)
+        part = part_of(j)
         return remote(raw_out.at[part], raw_near.at[part], near_send.at[j], near_recv.at[j], offset)
 
     def edge_copy(j, offset):
-        part = pl.ds(j * rows, rows)
+        part = part_of(j)
         return remote(raw_out.at[part], raw_far.at[part], edge_send.at[j], edge_recv.at[j], offset)
+
+    def pass_copy():
+        return remote(raw_near, raw_far, far_send.at[1], far_recv.at[1], 2)
 
     chunks = range(CHUNKS)
 
@@ -327,13 +336,8 @@
         for j in chunks:
             near_copy(j, -1).start()
 
-        @pl.when(down)
-        def _():
-            for j in chunks:
-                edge_copy(j, 1).start()
-
         for j in chunks:
-            part = pl.ds(j * rows, rows)
+            part = part_of(j)
             near_copy(j, 1).wait_recv()
 
             @pl.when(down)
@@ -352,32 +356,28 @@
             omega_copy().wait_send()
             field_copy(0).wait_send()
             field_copy(1).wait_send()
-            for j in chunks:
-                edge_copy(j, 1).wait_send()
 
     @pl.when(even)
     def _():
-        for load in loads[:6]:
+        for load in loads:
             load.wait()
         mean_own = look_up(0)
         means[0] = jnp.broadcast_to(mean_own, (8, 128))
-        pl.semaphore_wait(barrier, 1 + jnp.where(down, 1, 0) + jnp.where(up, 2, 0))
-
-        @pl.when(up)
-        def _():
-            mean_copy().start()
-
-        @pl.when(down)
-        def _():
-            omega_copy().start()
-
-        index_copy(1).start()
-        loads[6].wait()
         phase = phases(omega_of(0), mean_own)
         screen = screens(omega_of(0), 0, mean_own)
         step(own, work, (0, 1), phase, screen)
         first[...] = product(work)
-
+        pl.semaphore_wait(barrier, 1 + jnp.where(down, 1, 0) + jnp.where(up, 2, 0))
+
+        @pl.when(up)
+        def _():
+            mean_copy().start()
+
+        @pl.when(down)
+        def _():
+            omega_copy().start()
+
+        index_copy(1).start()
         index_copy(-1).wait_recv()
         mean_next = look_up(1)
         phase = phases(omega_of(0), mean_next)
@@ -390,8 +390,9 @@
         def _():
             mean_copy().wait_recv()
             phase = phases(omega_of(0), means[1, :1, :1])
-            for f, (b_re, b_im) in zip((0, 1), spectral(own, (0, 1), phase)):
-                made[f, 0], made[f, 1] = b_re, b_im
+            made[0, 0], made[0, 1] = spectral(own, (0,), phase)[0]
+            field_copy(0).start()
+            made[1, 0], made[1, 1] = spectral(own, (1,), phase)[0]
             for j in chunks:
                 tile_copy(j).start()
 
@@ -403,8 +404,22 @@
         part_copy(-1).wait_recv()
         first[...] = first[...] + part_in[...]
 
+        @pl.when(up)
+        def _():
+            field_copy(0).wait_recv()
+
         for j in chunks:
-            part = pl.ds(j * rows, rows)
+            part = part_of(j)
+            if j == 1:
+                for i in chunks:
+                    near_copy(i, -1).wait_recv()
+
+                @pl.when(down)
+                def _():
+                    field_copy(0).wait_send()
+                    for i in range(1):
+                        tile_copy(i).wait_send()
+                    pass_copy().start()
 
             @pl.when(up)
             def _():
@@ -414,23 +429,20 @@
             s_re, s_im = turned(0, got[0, 0, part], got[0, 1, part], screen)
             r_re, r_im = turned(1, got[1, 0, part], got[1, 1, part], screen)
             raw_out[part] = first[part] + s_re * r_re + s_im * r_im
-            fields_out[0, 0, 0, part], fields_out[0, 0, 1, part] = s_re, s_im
-            fields_out[0, 1, 0, part], fields_out[0, 1, 1, part] = r_re, r_im
-            near_copy(j, 1).start()
 
             @pl.when(up)
             def _():
                 edge_copy(j, -1).start()
 
-        for j in chunks:
-            part = pl.ds(j * rows, rows)
-            near_copy(j, -1).wait_recv()
-
-            @pl.when(up)
-            def _():
-                edge_copy(j, 1).wait_recv()
-
-            image_out[0, part] = raw_out[part] - 0.25 * (raw_near[part] + raw_far[part])
+            near_copy(j, 1).start()
+            fields_out[0, 0, 0, part], fields_out[0, 0, 1, part] = s_re, s_im
+            fields_out[0, 1, 0, part], fields_out[0, 1, 1, part] = r_re, r_im
+
+        @pl.when(up)
+        def _():
+            pass_copy().wait_recv()
+
+        image_out[0] = raw_out[...] - 0.25 * (raw_near[...] + raw_far[...])
 
         index_copy(1).wait_send()
         part_copy(1).wait_send()
@@ -440,7 +452,8 @@
         @pl.when(down)
         def _():
             omega_copy().wait_send()
-            for j in chunks:
+            pass_copy().wait_send()
+            for j in range(1, CHUNKS):
                 tile_copy(j).wait_send()
 
         @pl.when(up)

time: 23.7 us -> 22.2 us (0.937)
  Pallas kernels: 22.1 us -> 20.6 us
    pallas_call x1, Pallas kernels: 21.2 us -> 19.7 us  [body(): pl.pallas_call(functools.partial(kernel, count), out_shape=(pltpu.VMEM((1...]
where the time goes in v3:
time: 22.2 us; the launch traced here: 21.9 us
  Pallas kernels  20.6 us (93%)
  between operations  1.28 us (6%)
    pallas_call x1, Pallas kernels, body(): pl.pallas_call(functools.partial(kernel, count), out_shape=(pltpu.VMEM((1...  19.7 us
    pallas_call x1, Pallas kernels, body(): pl.pallas_call(store, out_shape=(jax.ShapeDtypeStruct((1, nx, ny), F32),...  0.85 us

profile of v3, /device:TPU:5, one launch (start us, length us, event | category | flops | bytes accessed | tf_op | source)
XLA Modules:
  0.0 21.9 jit_solution(16310599120583550440)
XLA Ops:
  1.3 19.7 %slabs.1 = (f32[1,128,256]{2,1,0:T(8,128)S(1)}, f32[1,2,2,128,256]{4,3,2,1,0:T(8,128)S(1)}) custom-call(f32[1,2,2,128,256]{4,3,2,1,0:T(8,128)} %fields.1, s32[1]{0:T(128)S(6)} %copy.9.freq, s32[1,128,256]{2,1,0:T(8,128)} %sidx.1, f32[256]{0:T(256)} %table.1, bf16[6,128,128]{2,1,0:T(8,128)(2,1)} %constant.4.clone.xs_in.ys_in, ...), custom_call_target="tpu_custom_call" | custom-call | tf_op jit(solution)/shard_map/slabs/pallas_call | solution.py:487
  21.0 0.8 %store.1 = (f32[1,128,256]{2,1,0:T(8,128)}, f32[1,2,2,128,256]{4,3,2,1,0:T(8,128)}) custom-call(f32[1,128,256]{2,1,0:T(8,128)S(1)} %get-tuple-element.4.image, f32[1,2,2,128,256]{4,3,2,1,0:T(8,128)S(1)} %get-tuple-element.5.fields), custom_call_target="tpu_custom_call" | custom-call | tf_op jit(solution)/shard_map/store/pallas_call | solution.py:534

commit v4 on v3

--- a/solution.py
+++ b/solution.py
@@ -363,21 +363,21 @@
             load.wait()
         mean_own = look_up(0)
         means[0] = jnp.broadcast_to(mean_own, (8, 128))
+        pl.semaphore_wait(barrier, 1 + jnp.where(down, 1, 0) + jnp.where(up, 2, 0))
+
+        @pl.when(up)
+        def _():
+            mean_copy().start()
+
+        @pl.when(down)
+        def _():
+            omega_copy().start()
+
+        index_copy(1).start()
         phase = phases(omega_of(0), mean_own)
         screen = screens(omega_of(0), 0, mean_own)
         step(own, work, (0, 1), phase, screen)
         first[...] = product(work)
-        pl.semaphore_wait(barrier, 1 + jnp.where(down, 1, 0) + jnp.where(up, 2, 0))
-
-        @pl.when(up)
-        def _():
-            mean_copy().start()
-
-        @pl.when(down)
-        def _():
-            omega_copy().start()
-
-        index_copy(1).start()
         index_copy(-1).wait_recv()
         mean_next = look_up(1)
         phase = phases(omega_of(0), mean_next)

time: 22.2 us -> 22.1 us (level)
  no operation moved by 1% of the time
where the time goes in v4:
time: 22.1 us; the launch traced here: 21.7 us
  Pallas kernels  20.4 us (92%)
  between operations  1.28 us (6%)
    pallas_call x1, Pallas kernels, body(): pl.pallas_call(functools.partial(kernel, count), out_shape=(pltpu.VMEM((1...  19.6 us
    pallas_call x1, Pallas kernels, body(): pl.pallas_call(store, out_shape=(jax.ShapeDtypeStruct((1, nx, ny), F32),...  0.85 us

profile of v4, /device:TPU:5, one launch (start us, length us, event | category | flops | bytes accessed | tf_op | source)
XLA Modules:
  0.0 21.7 jit_solution(16986893483999580086)
XLA Ops:
  1.3 19.6 %slabs.1 = (f32[1,128,256]{2,1,0:T(8,128)S(1)}, f32[1,2,2,128,256]{4,3,2,1,0:T(8,128)S(1)}) custom-call(f32[1,2,2,128,256]{4,3,2,1,0:T(8,128)} %fields.1, s32[1]{0:T(128)S(6)} %copy.9.freq, s32[1,128,256]{2,1,0:T(8,128)} %sidx.1, f32[256]{0:T(256)} %table.1, bf16[6,128,128]{2,1,0:T(8,128)(2,1)} %constant.4.clone.xs_in.ys_in, ...), custom_call_target="tpu_custom_call" | custom-call | tf_op jit(solution)/shard_map/slabs/pallas_call | solution.py:487
  20.9 0.8 %store.1 = (f32[1,128,256]{2,1,0:T(8,128)}, f32[1,2,2,128,256]{4,3,2,1,0:T(8,128)}) custom-call(f32[1,128,256]{2,1,0:T(8,128)S(1)} %get-tuple-element.4.image, f32[1,2,2,128,256]{4,3,2,1,0:T(8,128)S(1)} %get-tuple-element.5.fields), custom_call_target="tpu_custom_call" | custom-call | tf_op jit(solution)/shard_map/store/pallas_call | solution.py:534

commit v5 on v4

--- a/solution.py
+++ b/solution.py
@@ -93,6 +93,7 @@
     even = jnp.logical_not(odd)
     down = me + 2 < count
     up = me >= 2
+    straight = jnp.logical_and(up, lax.rem(me // 2, 2) == 0)
 
     def to(offset):
         return {"slab": jnp.clip(me + offset, 0, count - 1)}
@@ -275,8 +276,8 @@
         part = part_of(j)
         return remote(raw_out.at[part], raw_far.at[part], edge_send.at[j], edge_recv.at[j], offset)
 
-    def pass_copy():
-        return remote(raw_near, raw_far, far_send.at[1], far_recv.at[1], 2)
+    def pass_copy(source, offset):
+        return remote(source, raw_far, far_send.at[4], far_recv.at[4], offset)
 
     chunks = range(CHUNKS)
 
@@ -333,6 +334,10 @@
         step(work, fields_out.at[0], (1,), phase_1, screen_1)
         part_copy(1).wait_recv()
         raw_out[...] = first[...] + part_in[...] + product(fields_out.at[0])
+        @pl.when(jnp.logical_and(down, straight))
+        def _():
+            pass_copy(raw_out, 1).start()
+
         for j in chunks:
             near_copy(j, -1).start()
 
@@ -356,6 +361,10 @@
             omega_copy().wait_send()
             field_copy(0).wait_send()
             field_copy(1).wait_send()
+
+        @pl.when(jnp.logical_and(down, straight))
+        def _():
+            pass_copy(raw_out, 1).wait_send()
 
     @pl.when(even)
     def _():
@@ -414,12 +423,11 @@
                 for i in chunks:
                     near_copy(i, -1).wait_recv()
 
-                @pl.when(down)
+                @pl.when(jnp.logical_and(down, jnp.logical_not(straight)))
                 def _():
                     field_copy(0).wait_send()
-                    for i in range(1):
-                        tile_copy(i).wait_send()
-                    pass_copy().start()
+                    tile_copy(0).wait_send()
+                    pass_copy(raw_near, 2).start()
 
             @pl.when(up)
             def _():
@@ -440,7 +448,7 @@
 
         @pl.when(up)
         def _():
-            pass_copy().wait_recv()
+            pass_copy(raw_near, 2).wait_recv()
 
         image_out[0] = raw_out[...] - 0.25 * (raw_near[...] + raw_far[...])
 
@@ -452,9 +460,17 @@
         @pl.when(down)
         def _():
             omega_copy().wait_send()
-            pass_copy().wait_send()
             for j in range(1, CHUNKS):
                 tile_copy(j).wait_send()
+
+        @pl.when(jnp.logical_and(down, straight))
+        def _():
+            field_copy(0).wait_send()
+            tile_copy(0).wait_send()
+
+        @pl.when(jnp.logical_and(down, jnp.logical_not(straight)))
+        def _():
+            pass_copy(raw_near, 2).wait_send()
 
         @pl.when(up)
         def _():
@@ -514,8 +530,8 @@
             pltpu.VMEM(plane, F32),
             pltpu.VMEM(plane, F32),
             dma((7,)),
-            dma((4,)),
-            dma((4,)),
+            dma((5,)),
+            dma((5,)),
             dma((CHUNKS,)),
             dma((CHUNKS,)),
             dma((2,)),

time: 22.1 us -> 21.9 us (level)
  no operation moved by 1% of the time
where the time goes in v5:
time: 21.9 us; the launch traced here: 21.7 us
  Pallas kernels  20.4 us (93%)
  between operations  1.28 us (6%)
    pallas_call x1, Pallas kernels, body(): pl.pallas_call(functools.partial(kernel, count), out_shape=(pltpu.VMEM((1...  19.6 us
    pallas_call x1, Pallas kernels, body(): pl.pallas_call(store, out_shape=(jax.ShapeDtypeStruct((1, nx, ny), F32),...  0.85 us

profile of v5, /device:TPU:5, one launch (start us, length us, event | category | flops | bytes accessed | tf_op | source)
XLA Modules:
  0.0 21.7 jit_solution(14230283642371061724)
XLA Ops:
  1.3 19.6 %slabs.1 = (f32[1,128,256]{2,1,0:T(8,128)S(1)}, f32[1,2,2,128,256]{4,3,2,1,0:T(8,128)S(1)}) custom-call(f32[1,2,2,128,256]{4,3,2,1,0:T(8,128)} %fields.1, s32[1]{0:T(128)S(6)} %copy.9.freq, s32[1,128,256]{2,1,0:T(8,128)} %sidx.1, f32[256]{0:T(256)} %table.1, bf16[6,128,128]{2,1,0:T(8,128)(2,1)} %constant.4.clone.xs_in.ys_in, ...), custom_call_target="tpu_custom_call" | custom-call | tf_op jit(solution)/shard_map/slabs/pallas_call | solution.py:503
  20.9 0.8 %store.1 = (f32[1,128,256]{2,1,0:T(8,128)}, f32[1,2,2,128,256]{4,3,2,1,0:T(8,128)}) custom-call(f32[1,128,256]{2,1,0:T(8,128)S(1)} %get-tuple-element.4.image, f32[1,2,2,128,256]{4,3,2,1,0:T(8,128)S(1)} %get-tuple-element.5.fields), custom_call_target="tpu_custom_call" | custom-call | tf_op jit(solution)/shard_map/store/pallas_call | solution.py:550

commit v6 on v5

--- a/solution.py
+++ b/solution.py
@@ -419,7 +419,7 @@
 
         for j in chunks:
             part = part_of(j)
-            if j == 1:
+            if j == 2:
                 for i in chunks:
                     near_copy(i, -1).wait_recv()
 
@@ -427,6 +427,7 @@
                 def _():
                     field_copy(0).wait_send()
                     tile_copy(0).wait_send()
+                    tile_copy(1).wait_send()
                     pass_copy(raw_near, 2).start()
 
             @pl.when(up)
@@ -442,7 +443,10 @@
             def _():
                 edge_copy(j, -1).start()
 
-            near_copy(j, 1).start()
+            if j == CHUNKS - 1:
+                for i in chunks:
+                    near_copy(i, 1).start()
+
             fields_out[0, 0, 0, part], fields_out[0, 0, 1, part] = s_re, s_im
             fields_out[0, 1, 0, part], fields_out[0, 1, 1, part] = r_re, r_im
 
@@ -460,13 +464,14 @@
         @pl.when(down)
         def _():
             omega_copy().wait_send()
-            for j in range(1, CHUNKS):
+            for j in range(2, CHUNKS):
                 tile_copy(j).wait_send()
 
         @pl.when(jnp.logical_and(down, straight))
         def _():
             field_copy(0).wait_send()
             tile_copy(0).wait_send()
+            tile_copy(1).wait_send()
 
         @pl.when(jnp.logical_and(down, jnp.logical_not(straight)))
         def _():

time: 21.9 us -> 21.9 us (level)
  no operation moved by 1% of the time
where the time goes in v6:
time: 21.9 us; the launch traced here: 21.7 us
  Pallas kernels  20.4 us (93%)
  between operations  1.28 us (6%)
    pallas_call x1, Pallas kernels, body(): pl.pallas_call(functools.partial(kernel, count), out_shape=(pltpu.VMEM((1...  19.6 us
    pallas_call x1, Pallas kernels, body(): pl.pallas_call(store, out_shape=(jax.ShapeDtypeStruct((1, nx, ny), F32),...  0.85 us

profile of v6, /device:TPU:5, one launch (start us, length us, event | category | flops | bytes accessed | tf_op | source)
XLA Modules:
  0.0 21.7 jit_solution(2989211209528588935)
XLA Ops:
  1.3 19.6 %slabs.1 = (f32[1,128,256]{2,1,0:T(8,128)S(1)}, f32[1,2,2,128,256]{4,3,2,1,0:T(8,128)S(1)}) custom-call(f32[1,2,2,128,256]{4,3,2,1,0:T(8,128)} %fields.1, s32[1]{0:T(128)S(6)} %copy.9.freq, s32[1,128,256]{2,1,0:T(8,128)} %sidx.1, f32[256]{0:T(256)} %table.1, bf16[6,128,128]{2,1,0:T(8,128)(2,1)} %constant.4.clone.xs_in.ys_in, ...), custom_call_target="tpu_custom_call" | custom-call | tf_op jit(solution)/shard_map/slabs/pallas_call | solution.py:508
  20.9 0.8 %store.1 = (f32[1,128,256]{2,1,0:T(8,128)}, f32[1,2,2,128,256]{4,3,2,1,0:T(8,128)}) custom-call(f32[1,128,256]{2,1,0:T(8,128)S(1)} %get-tuple-element.4.image, f32[1,2,2,128,256]{4,3,2,1,0:T(8,128)S(1)} %get-tuple-element.5.fields), custom_call_target="tpu_custom_call" | custom-call | tf_op jit(solution)/shard_map/store/pallas_call | solution.py:555

commit v7 on v5

--- a/solution.py
+++ b/solution.py
@@ -442,7 +442,10 @@
             def _():
                 edge_copy(j, -1).start()
 
-            near_copy(j, 1).start()
+            if j == CHUNKS - 1:
+                for i in chunks:
+                    near_copy(i, 1).start()
+
             fields_out[0, 0, 0, part], fields_out[0, 0, 1, part] = s_re, s_im
             fields_out[0, 1, 0, part], fields_out[0, 1, 1, part] = r_re, r_im
 

time: 21.9 us -> 21.9 us (level)
  no operation moved by 1% of the time
where the time goes in v7:
time: 21.9 us; the launch traced here: 21.7 us
  Pallas kernels  20.4 us (93%)
  between operations  1.28 us (6%)
    pallas_call x1, Pallas kernels, body(): pl.pallas_call(functools.partial(kernel, count), out_shape=(pltpu.VMEM((1...  19.6 us
    pallas_call x1, Pallas kernels, body(): pl.pallas_call(store, out_shape=(jax.ShapeDtypeStruct((1, nx, ny), F32),...  0.85 us

profile of v7, /device:TPU:5, one launch (start us, length us, event | category | flops | bytes accessed | tf_op | source)
XLA Modules:
  0.0 21.7 jit_solution(6850975628301327213)
XLA Ops:
  1.3 19.6 %slabs.1 = (f32[1,128,256]{2,1,0:T(8,128)S(1)}, f32[1,2,2,128,256]{4,3,2,1,0:T(8,128)S(1)}) custom-call(f32[1,2,2,128,256]{4,3,2,1,0:T(8,128)} %fields.1, s32[1]{0:T(128)S(6)} %copy.9.freq, s32[1,128,256]{2,1,0:T(8,128)} %sidx.1, f32[256]{0:T(256)} %table.1, bf16[6,128,128]{2,1,0:T(8,128)(2,1)} %constant.4.clone.xs_in.ys_in, ...), custom_call_target="tpu_custom_call" | custom-call | tf_op jit(solution)/shard_map/slabs/pallas_call | solution.py:506
  20.9 0.8 %store.1 = (f32[1,128,256]{2,1,0:T(8,128)}, f32[1,2,2,128,256]{4,3,2,1,0:T(8,128)}) custom-call(f32[1,128,256]{2,1,0:T(8,128)S(1)} %get-tuple-element.4.image, f32[1,2,2,128,256]{4,3,2,1,0:T(8,128)S(1)} %get-tuple-element.5.fields), custom_call_target="tpu_custom_call" | custom-call | tf_op jit(solution)/shard_map/store/pallas_call | solution.py:553

commit v8 on v7

--- a/solution.py
+++ b/solution.py
@@ -98,6 +98,32 @@
     def to(offset):
         return {"slab": jnp.clip(me + offset, 0, count - 1)}
 
+    barrier = pltpu.get_barrier_semaphore()
+
+    @pl.when(odd)
+    def _():
+        pl.semaphore_signal(barrier, inc=1, device_id=to(-1))
+
+        @pl.when(down)
+        def _():
+            pl.semaphore_signal(barrier, inc=1, device_id=to(1))
+
+    @pl.when(even)
+    def _():
+        pl.semaphore_signal(barrier, inc=1, device_id=to(1))
+
+        @pl.when(up)
+        def _():
+            pl.semaphore_signal(barrier, inc=1, device_id=to(-1))
+
+    @pl.when(down)
+    def _():
+        pl.semaphore_signal(barrier, inc=1, device_id=to(2))
+
+    @pl.when(up)
+    def _():
+        pl.semaphore_signal(barrier, inc=1, device_id=to(-2))
+
     loads = [
         pltpu.make_async_copy(fields.at[0, 0], own.at[0], in_sems.at[0]),
         pltpu.make_async_copy(xs_in, xs, in_sems.at[1]),
@@ -109,32 +135,6 @@
     ]
     for load in loads:
         load.start()
-
-    barrier = pltpu.get_barrier_semaphore()
-
-    @pl.when(odd)
-    def _():
-        pl.semaphore_signal(barrier, inc=1, device_id=to(-1))
-
-        @pl.when(down)
-        def _():
-            pl.semaphore_signal(barrier, inc=1, device_id=to(1))
-
-    @pl.when(even)
-    def _():
-        pl.semaphore_signal(barrier, inc=1, device_id=to(1))
-
-        @pl.when(up)
-        def _():
-            pl.semaphore_signal(barrier, inc=1, device_id=to(-1))
-
-    @pl.when(down)
-    def _():
-        pl.semaphore_signal(barrier, inc=1, device_id=to(2))
-
-    @pl.when(up)
-    def _():
-        pl.semaphore_signal(barrier, inc=1, device_id=to(-2))
 
     row = lax.broadcasted_iota(jnp.int32, (nx, half), 0)
     wave_x = jnp.where(row < (nx + 1) // 2, row, row - nx).astype(F32) * (2.0 * math.pi / nx)

time: 21.9 us -> 21.9 us (level)
  no operation moved by 1% of the time
where the time goes in v8:
time: 21.9 us; the launch traced here: 21.8 us
  Pallas kernels  20.5 us (94%)
  between operations  1.28 us (6%)
    pallas_call x1, Pallas kernels, body(): pl.pallas_call(functools.partial(kernel, count), out_shape=(pltpu.VMEM((1...  19.7 us
    pallas_call x1, Pallas kernels, body(): pl.pallas_call(store, out_shape=(jax.ShapeDtypeStruct((1, nx, ny), F32),...  0.85 us

profile of v8, /device:TPU:5, one launch (start us, length us, event | category | flops | bytes accessed | tf_op | source)
XLA Modules:
  0.0 21.8 jit_solution(14941233615170230441)
XLA Ops:
  1.3 19.7 %slabs.1 = (f32[1,128,256]{2,1,0:T(8,128)S(1)}, f32[1,2,2,128,256]{4,3,2,1,0:T(8,128)S(1)}) custom-call(f32[1,2,2,128,256]{4,3,2,1,0:T(8,128)} %fields.1, s32[1]{0:T(128)S(6)} %copy.9.freq, s32[1,128,256]{2,1,0:T(8,128)} %sidx.1, f32[256]{0:T(256)} %table.1, bf16[6,128,128]{2,1,0:T(8,128)(2,1)} %constant.4.clone.xs_in.ys_in, ...), custom_call_target="tpu_custom_call" | custom-call | tf_op jit(solution)/shard_map/slabs/pallas_call | solution.py:506
  20.9 0.8 %store.1 = (f32[1,128,256]{2,1,0:T(8,128)}, f32[1,2,2,128,256]{4,3,2,1,0:T(8,128)}) custom-call(f32[1,128,256]{2,1,0:T(8,128)S(1)} %get-tuple-element.4.image, f32[1,2,2,128,256]{4,3,2,1,0:T(8,128)S(1)} %get-tuple-element.5.fields), custom_call_target="tpu_custom_call" | custom-call | tf_op jit(solution)/shard_map/store/pallas_call | solution.py:553
